TPU v7x, 128 devices: a whole 4x4x4 slice. The times are simulated.
128 devices in a mesh: piece: 32 (over y, x, core), col: 4 (over z).
Axes of the slice: x: 4, y: 4, z: 4, core: 2. Of those that a mesh axis runs over, the one named last changes fastest.
Arguments:
- positions: float32 [3, 4096, 128], P(None, 'piece'), as said below
- phase: int32 [4096, 128], P('piece'), may hold values from 0 to 2
- neighbours: int32 [4096, 28], P('piece', 'col'), may hold values from -1 to 4095, as said below
- counts: int32 [32], replicated, may hold values from 64 to 128, as said below
- phase_density: float32 [3], replicated, may hold values from 0.1 to 1
- right_side: float32 [4096, 128], P(('piece', 'col')), may hold values from -6 to 6
Outputs:
- solution_field: float32 [4096, 128], P(('piece', 'col'))
- residual: float32 [4096, 128], P(('piece', 'col'))
Inputs may be any that keep to these rules, and one draw needn't show every extreme that they name: `neighbours`: the slots of each piece at or past its count hold no block. Live blocks, taken in slot order piece after piece, form layers of 16 blocks in Morton order of a 4 x 4 grid. Block q lists n exactly when n lists q; every listed block lies on q's own piece or the piece just before or after it, and its place in that order of live blocks differs from q's by less than 32; empty slots and the last column list only -1. `counts`: some piece holds exactly 128 live blocks. `positions`: the particles of one live block lie in one unit cell; particles of two live blocks that do not list each other are 1 or more apart.
All inputs are finite; a program needn't handle non-finite values.
Results may differ from a plain program's by a relative error of at most 0.0003.
Values sent between devices are 32-bit elements; how exact they have to be, the bound alone decides.
A program may use at most 64 MiB of HBM per device.

v0:
```python
import math

import jax
import jax.numpy as jnp
from jax import lax
from jax.sharding import PartitionSpec as P

ITERS = 2


def padded(cells, sides, width):
    for axis, dim in sides:
        count = lax.axis_size(axis)
        ends = count - 1
        head = lax.slice_in_dim(cells, 0, width, axis=dim)
        tail = lax.slice_in_dim(cells, cells.shape[dim] - width, cells.shape[dim], axis=dim)
        cells = jnp.concatenate(
            [
                lax.ppermute(tail, axis, [(i, (i + 1) % count) for i in range(ends)]),
                cells,
                lax.ppermute(head, axis, [((i + 1) % count, i) for i in range(ends)]),
            ],
            axis=dim,
        )
    return cells


def fetch_phase_density(phase, phase_density):
    labels = jnp.arange(3, dtype=jnp.int32)
    return jnp.sum(jnp.where(phase[..., None] == labels, phase_density, 0.0), axis=-1)


def pair_term(own_pos, own_rho, own_ids, slot_ids, hood_state, hood_field, base):
    valid = slot_ids >= 0
    where_at = jnp.clip(slot_ids - base, 0, hood_field.shape[0] - 1)
    other = hood_state[:, where_at]
    remote = hood_field[where_at]
    squared = jnp.zeros((own_rho.shape[0], own_rho.shape[1], own_rho.shape[1]), jnp.float32)
    for component in range(3):
        slot_displacement = own_pos[component][:, :, None] - other[component][:, None, :]
        squared = squared + slot_displacement * slot_displacement
    kernel = jnp.square(jnp.maximum(1.0 - squared, 0.0)) / (squared + 0.01)
    weight = 2.0 / (own_rho[:, :, None] + other[3][:, None, :])
    particles = jnp.arange(own_rho.shape[1], dtype=jnp.int32)
    same = (slot_ids == own_ids)[:, None, None] & (particles[:, None] == particles[None, :])[None]
    keep = valid[:, None, None] & jnp.logical_not(same)
    tile = jnp.where(keep, kernel * weight / own_rho.shape[1], 0.0)
    return jnp.einsum("gij,gj->gi", tile, remote, precision=lax.Precision.HIGHEST)


def body(positions, phase, neighbours, counts, phase_density, right_side):
    capacity = positions.shape[1]
    per_block = positions.shape[2]
    columns = lax.axis_size("col")
    share = capacity // columns
    piece = lax.axis_index("piece")
    column = lax.axis_index("col")
    density = fetch_phase_density(phase, phase_density)
    state = jnp.concatenate([positions, density[None]], 0)
    filled = counts[piece]
    hood_state = padded(state, (("piece", 1),), capacity)

    def remap(ids):
        return jnp.where(ids >= 0, ids - (piece - 1) * capacity, -1)

    hood_size = hood_state.shape[1]
    live = jnp.arange(capacity, dtype=jnp.int32) < filled
    group = math.gcd(16, capacity)
    ngroup = capacity // group

    def group_sum(field_hood, start):
        own_pos = lax.dynamic_slice_in_dim(positions, start, group, 1)
        own_rho = lax.dynamic_slice_in_dim(density, start, group, 0)
        own_ids = capacity + start + jnp.arange(group, dtype=jnp.int32)
        lists = remap(lax.dynamic_slice_in_dim(neighbours, start, group, 0))
        running = jnp.zeros((group, per_block), jnp.float32)
        for neighbour_slot in range(lists.shape[1]):
            running = running + pair_term(
                own_pos, own_rho, own_ids, lists[:, neighbour_slot], hood_state, field_hood, 0
            )
        return running

    def own_terms(field_hood):
        starts = jnp.arange(ngroup, dtype=jnp.int32) * group
        output_blocks = lax.map(lambda start: group_sum(field_hood, start), starts)
        return output_blocks.reshape(capacity, per_block)

    def mine(values):
        return lax.dynamic_slice_in_dim(values, column * share, share, 0)

    def totals(part_sum):
        return lax.psum_scatter(part_sum, "col", scatter_dimension=0, tiled=True)

    source = jnp.where(mine(live)[:, None], right_side, 0.0)
    rho_vector = mine(density)

    def inner(first, second):
        return jnp.sum(first * second)

    diagonal = 1.0 / rho_vector + totals(own_terms(jnp.ones((hood_size, per_block), jnp.float32)))
    solution_field = jnp.zeros_like(source)
    residual = source

    def weighted_sum(first, second):
        return lax.psum(inner(first, second), ("piece", "col"))

    precond = residual / diagonal
    direction = precond
    weighted = weighted_sum(residual, precond)
    for step in range(ITERS):
        image = diagonal * direction - totals(
            own_terms(
                padded(
                    lax.all_gather(direction, "col", axis=0, tiled=True), (("piece", 0),), capacity
                )
            )
        )
        advance = weighted / lax.psum(inner(direction, image), ("piece", "col"))
        solution_field = solution_field + advance * direction
        residual = residual - advance * image
        precond = residual / diagonal
        weighted_next = weighted_sum(residual, precond)
        direction = precond + weighted_next / weighted * direction
        weighted = weighted_next
    return (solution_field, residual)


def solution(mesh):
    placed = (
        P(None, "piece", None),
        P("piece", None),
        P("piece", "col"),
        P(),
        P(),
        P(("piece", "col"), None),
    )
    return jax.shard_map(
        body,
        mesh=mesh,
        in_specs=placed,
        out_specs=(P(("piece", "col"), None), P(("piece", "col"), None)),
        check_vma=False,
    )
```

profile of v0, /device:TPU:1, one launch (start us, length us, event | category | flops | bytes accessed | tf_op | source)
XLA Modules:
  0.0 1112.0 jit_solution(1713811244418528213)
XLA Ops:
  8.5 4.5 collective-permute-start
  16.3 4.4 collective-permute-done.1
  21.7 257.3 %while.36 = (s32[]{:T(128)}, f32[8,16,128]{2,1,0:T(8,128)S(1)}, s32[8]{0:T(128)S(1)}, s32[128,7]{0,1:T(8,128)S(1)}, s32[]{:T(128)}, /*index=5*/f32[3,128,128]{2,...) while((s32[]{:T(128)}, f32[8,16,128]{2,1,0:T(8,128)S(1)}, ...), condition=%wide.region_2.3_spmd, body=%wide.region_1.2_spmd.sunk | while | flops 60592136 | bytes 2097327 | solution.py:85
  26.3 2.9 fusion.1081
  58.4 2.9 fusion.1081
  90.6 2.9 fusion.1081
  122.8 2.9 fusion.1081
  154.9 2.9 fusion.1081
  187.1 2.9 fusion.1081
  219.3 2.9 fusion.1081
  281.0 20.7 %reduce-scatter.4.cloned.1.call-done = f32[32,128]{1,0:T(8,128)} async-done(((f32[128,128]{1,0:T(8,128)}), f32[32,128]{1,0:T(8,128)}) %reduce-scatter.4.cloned.1.call-update) | async-done | bytes 16400 | tf_op jit(solution)/shard_map/reduce_scatter | solution.py:92
  302.5 9.0 all_gather.6
  311.5 8.8 collective-permute-start.2
  322.4 3.5 collective-permute-done.3
  325.9 257.1 %while.37 = (s32[]{:T(128)}, f32[8,16,128]{2,1,0:T(8,128)S(1)}, s32[8]{0:T(128)S(1)}, s32[128,7]{0,1:T(8,128)S(1)}, s32[]{:T(128)}, /*index=5*/f32[3,128,128]{2,...) while((s32[]{:T(128)}, f32[8,16,128]{2,1,0:T(8,128)S(1)}, ...), condition=%wide.region_7.8_spmd, body=%wide.region_6.7_spmd.sunk | while | flops 60592136 | bytes 1900715 | solution.py:85
  394.8 2.9 fusion.1110
  426.9 2.9 fusion.1110
  459.1 2.9 fusion.1110
  583.8 19.2 %reduce-scatter.6.cloned.1.call-done = f32[32,128]{1,0:T(8,128)} async-done(((f32[128,128]{1,0:T(8,128)}), f32[32,128]{1,0:T(8,128)}) %reduce-scatter.6.cloned.1.call-update) | async-done | bytes 16400 | tf_op jit(solution)/shard_map/reduce_scatter | solution.py:92
  604.5 66.9 %all-reduce = (f32[]{:T(128)}, f32[]{:T(128)}) all-reduce(f32[]{:T(128)} %get-tuple-element.316, f32[]{:T(128)} %get-tuple-element.315), channel_id=1, replica_groups=mesh['piece'=32,'col'=4] {'piece','col'}, use_global_device_ids=true, to_apply=%region_5.6 | all-reduce | flops 2 | bytes 16 | tf_op jit(solution)/shard_map/psum | solution.py:105
  673.4 62.5 %psum.30 = f32[]{:T(128)} all-reduce(f32[]{:T(128)} %get-tuple-element.371), channel_id=1, replica_groups=mesh['piece'=32,'col'=4] {'piece','col'}, use_global_device_ids=true, to_apply=%region_12.13 | all-reduce | flops 1 | bytes 8 | tf_op jit(solution)/shard_map/psum | solution.py:105
  737.2 9.0 all_gather.7
  746.3 6.3 collective-permute-start.4
  754.8 3.4 collective-permute-done.5
  758.2 257.2 %while.38 = (s32[]{:T(128)}, f32[8,16,128]{2,1,0:T(8,128)S(1)}, s32[8]{0:T(128)S(1)}, s32[128,7]{0,1:T(8,128)S(1)}, s32[]{:T(128)}, /*index=5*/f32[3,128,128]{2,...) while((s32[]{:T(128)}, f32[8,16,128]{2,1,0:T(8,128)S(1)}, ...), condition=%wide.region_14.15_spmd, body=%wide.region_13.14_spmd.sunk | while | flops 60592136 | bytes 1900715 | solution.py:85
  794.9 2.9 fusion.1139
  859.2 2.9 fusion.1139
  891.4 2.9 fusion.1139
  923.5 2.9 fusion.1139
  955.7 2.9 fusion.1139
  1016.0 19.2 %reduce-scatter.8.cloned.1.call-done = f32[32,128]{1,0:T(8,128)} async-done(((f32[128,128]{1,0:T(8,128)}), f32[32,128]{1,0:T(8,128)}) %reduce-scatter.8.cloned.1.call-update) | async-done | bytes 16400 | tf_op jit(solution)/shard_map/reduce_scatter | solution.py:92
  1036.6 66.8 %psum.31 = f32[]{:T(128)} all-reduce(f32[]{:T(128)} %multiply_reduce_fusion), channel_id=1, replica_groups=mesh['piece'=32,'col'=4] {'piece','col'}, use_global_device_ids=true, to_apply=%region_17.18 | all-reduce | flops 1 | bytes 8 | tf_op jit(solution)/shard_map/psum | solution.py:118
  (1004 shorter events, 698.6 us)
Async XLA Ops:
  7.2 1.1 copy-start.6
  7.2 1.1 copy-start.8
  7.2 294.5 %reduce-scatter.4.cloned.1.call-start = ((), (), s32[]{:S(2)}) async-start(), calls=%async_computation.3 | async-start | bytes 81920 | tf_op jit(solution)/shard_map/reduce_scatter | solution.py:92
  8.5 7.8 collective-permute-start
  13.0 7.7 collective-permute-start.1
  21.0 0.7 copy-start
  21.7 258.0 %copy-start.9 = (s32[32]{0:T(128)S(1)}, s32[32]{0:T(128)}, u32[]{:S(2)}) copy-start(s32[32]{0:T(128)} %param.15) | copy-start | bytes 388
  279.0 0.6 copy-start.2
  279.6 22.1 %copy-start.4 = (f32[32,128]{1,0:T(8,128)S(1)}, f32[32,128]{1,0:T(8,128)}, u32[]{:S(2)}) copy-start(f32[32,128]{1,0:T(8,128)} %param.17) | copy-start | bytes 49156
  279.6 323.3 %reduce-scatter.6.cloned.1.call-start = ((), (), s32[]{:S(2)}) async-start(), calls=%async_computation.4 | async-start | bytes 81920 | tf_op jit(solution)/shard_map/reduce_scatter | solution.py:92
  311.5 10.9 collective-permute-start.2
  320.3 5.6 collective-permute-start.3
  583.1 0.6 copy-start.3
  583.7 451.5 %reduce-scatter.8.cloned.1.call-start = ((), (), s32[]{:S(2)}) async-start(), calls=%async_computation.5 | async-start | bytes 81920 | tf_op jit(solution)/shard_map/reduce_scatter | solution.py:92
  603.0 69.7 %copy-start.7 = (f32[32,128]{1,0:T(8,128)S(1)}, f32[32,128]{1,0:T(8,128)}, u32[]{:S(2)}) copy-start(f32[32,128]{1,0:T(8,128)} %reduce-scatter.6.cloned.1.call-done) | copy-start | bytes 49156
  746.3 8.5 collective-permute-start.4
  752.6 5.6 collective-permute-start.5
  1015.4 0.6 copy-start.1
  1035.2 69.6 %copy-start.5 = (f32[32,128]{1,0:T(8,128)S(1)}, f32[32,128]{1,0:T(8,128)}, u32[]{:S(2)}) copy-start(f32[32,128]{1,0:T(8,128)} %reduce-scatter.8.cloned.1.call-done) | copy-start | bytes 49156
Sparse Core Ops, SparseCore 0:
  279.8 21.9 reduce-scatter.3
  583.8 19.0 reduce-scatter.5
  1016.2 19.0 reduce-scatter.7
where the time goes:
time: 1120 us; the launch traced here: 1110 us
  matrix products  488 us (44%)
  local copies, waits for them, and re-layouts  236 us (21%)
  blocking collectives  214 us (19%)
  waiting for transfers between devices  71.8 us (6%)
  loops' own time  47.6 us (4%)
  starting transfers between devices  25.9 us (2%)
  between operations  18 us (2%)
    dot_general x168, matrix products, pair_term(): jnp.einsum('gij,gj->gi', tile, remote, precision=lax.Precision.HIGHEST)  488 us
    psum x2, blocking collectives, weighted_sum(): return lax.psum(inner(first, second), ('piece', 'col'))  129 us
    gather x168, local copies, waits for them, and re-layouts, pair_term(): other = hood_state[:, where_at]  101 us
    gather x168, local copies, waits for them, and re-layouts, pair_term(): remote = hood_field[where_at]  94.4 us
    psum x1, blocking collectives, body(): advance = weighted / lax.psum(inner(direction, image), ('piece', 'col'))  66.8 us
    reduce_scatter x3, waiting for transfers between devices, totals(): return lax.psum_scatter(part_sum, 'col', scatter_dimension=0, tiled=True)  59.1 us
    another operation x3, loops' own time, own_terms(): output_blocks = lax.map(lambda start: group_sum(field_hood, start), starts)  47.6 us
  transfers between devices with their start and end apart: 9, of which 7 were waited for; matrix products, arithmetic and copies ran while one was open for 0% of the time, Pallas kernels for 0%

commit v1 on v0

v1 whole, which is shorter than its diff:
```python
import functools

import jax
import jax.numpy as jnp
import numpy as np
from jax import lax
from jax.experimental import pallas as pl
from jax.experimental.pallas import tpu as pltpu
from jax.sharding import PartitionSpec as P

MESH = pl.DeviceIdType.MESH
BLK = 128
CAP = 128
LAYER = 16
SHARE = 32
FAR = 1.0e4
FAR_NULL = 2.0e4
STATE_NULL = 192
FIELD_NULL = 256


def layer_cells():
    place = []
    for code in range(LAYER):
        across = code % 2 + 2 * (code // 4 % 2)
        along = code // 2 % 2 + 2 * (code // 8 % 2)
        place.append((across, along))
    near = []
    for code in range(LAYER):
        others = [
            other
            for other in range(LAYER)
            if other != code
            and abs(place[other][0] - place[code][0]) <= 1
            and abs(place[other][1] - place[code][1]) <= 1
        ]
        near.append([code] + others)
    return near


NEAR = layer_cells()
CELLS = sorted(range(LAYER), key=lambda code: (len(NEAR[code]), code))


def tile_plan():
    rows, groups = [], []
    own_cell, own_half = [], []
    for degree in (4, 6, 9):
        cells = [code for code in CELLS if len(NEAR[code]) == degree]
        groups.append((degree, len(own_cell), 2 * len(cells), len(rows)))
        for code in cells:
            for half in range(2):
                own_cell.append(code)
                own_half.append(half)
                for kind in range(3):
                    for other in NEAR[code]:
                        rows.append((code, half, kind, other))
    return np.array(rows, np.int32), groups, np.array(own_cell, np.int32), np.array(own_half, np.int32)


ROWS, GROUPS, OWN_CELL, OWN_HALF = tile_plan()
TILES = ROWS.shape[0]
UNITS = 2 * LAYER
RANK_OF = np.zeros((LAYER,), np.int32)
for _rank, _code in enumerate(CELLS):
    RANK_OF[_code] = _rank


def tables(counts, piece, column):
    lanes = jnp.arange(counts.shape[0], dtype=jnp.int32)
    start = jnp.sum(jnp.where(lanes < piece, counts, 0))
    total = jnp.sum(counts)
    filled = jnp.sum(jnp.where(lanes == piece, counts, 0))
    before = jnp.sum(jnp.where(lanes == piece - 1, counts, 0))
    first = start + SHARE * column

    def local(cell, half):
        return (cell - first) % LAYER + LAYER * half

    cell, half, kind, other = (jnp.asarray(ROWS[:, i]) for i in range(4))
    own = local(cell, half)
    mate = local(other, half)
    level = (first + own) // LAYER
    lift = (first + mate) // LAYER - level
    step = jnp.where(
        kind == 0, lift, jnp.where(kind == 1, jnp.where(lift == -1, 0, -1), jnp.where(lift == 1, 0, 1))
    )
    order = LAYER * (level + step) + other
    slot = order - start
    good = (order >= 0) & (order < total) & (SHARE * column + own < filled)
    state_at = jnp.where(slot < filled, SHARE + slot, SHARE + CAP + slot - filled)
    state_at = jnp.where(good, state_at, STATE_NULL)
    field_at = jnp.where(
        slot < 0,
        before + slot - SHARE,
        jnp.where(slot < filled, 3 * SHARE + slot, 3 * SHARE + CAP + slot - filled),
    )
    field_at = jnp.where(good, field_at, FIELD_NULL)
    units = local(jnp.asarray(OWN_CELL), jnp.asarray(OWN_HALF))
    spots = jnp.arange(UNITS, dtype=jnp.int32)
    cell_of = (first + spots) % LAYER
    rank_of = jnp.sum(
        jnp.where(cell_of[:, None] == jnp.arange(LAYER)[None], jnp.asarray(RANK_OF)[None], 0), axis=1
    )
    unit_of = 2 * rank_of + spots // LAYER
    return jnp.concatenate([state_at, field_at, units, unit_of, filled[None]]).astype(jnp.int32)


FIELD_TAB = TILES
UNIT_TAB = 2 * TILES
SPOT_TAB = 2 * TILES + UNITS
FILLED_TAB = 2 * TILES + 2 * UNITS


def kernel(
    pieces, columns,
    tab, dens, pos_ref, phase_ref, near_ref, rhs_ref,
    x_ref, r_ref,
    state, spread, tiles, listed, listed_in, head, tail, density,
    own_z, own_t, hood_z, hood_t, rowbuf, diag, y0, y1, moments, stage_a, stage_b,
    state_send, state_recv, list_send, list_recv, z_send, z_recv, t_send, t_recv, a_send, a_recv, b_send, b_recv,
):
    piece = lax.axis_index("piece")
    column = lax.axis_index("col")
    after = lax.rem(piece + 1, pieces)
    ahead = lax.rem(piece + pieces - 1, pieces)
    core = lax.rem(piece, 2)
    chip = piece // 2
    rank_a = column * 2 + core

    def member_a(rank):
        return (chip * 2 + lax.rem(rank, 2), rank // 2)

    def member_b(rank):
        return (rank * 2 + core, column)

    barrier = pltpu.get_barrier_semaphore()

    def greet(target):
        pl.semaphore_signal(barrier, inc=1, device_id=target, device_id_type=MESH)

    greet((after, column))
    greet((ahead, column))
    for step in range(1, columns):
        greet((piece, lax.rem(column + step, columns)))
    for step in range(1, 8):
        greet(member_a(lax.rem(rank_a + step, 8)))
    for step in range(1, 16):
        greet(member_b(lax.rem(chip + step, 16)))

    @pl.when(column == 0)
    def _():
        for other in range(1, columns):
            greet((ahead, other))

    @pl.when(column > 0)
    def _():
        greet((after, 0))

    filled = tab[FILLED_TAB]
    slots = lax.broadcasted_iota(jnp.int32, (CAP, BLK), 0)
    live = slots < filled
    for axis in range(3):
        state[axis, SHARE : SHARE + CAP, :] = jnp.where(live, pos_ref[axis], FAR)
        state[axis, STATE_NULL : STATE_NULL + 8, :] = jnp.full((8, BLK), FAR_NULL, jnp.float32)
    phase = phase_ref[...]
    scaled = jnp.where(phase == 0, dens[0], jnp.where(phase == 1, dens[1], dens[2])) * 64.0
    state[3, SHARE : SHARE + CAP, :] = jnp.where(live, scaled, 64.0)
    state[3, STATE_NULL : STATE_NULL + 8, :] = jnp.full((8, BLK), 64.0, jnp.float32)

    near = near_ref[...]
    me_at = lax.broadcasted_iota(jnp.int32, near.shape, 0) + piece * CAP
    hits = jnp.sum(jnp.where(near == me_at, 1.0, 0.0), axis=1, keepdims=True)
    listed[...] = jnp.broadcast_to(hits, (CAP, BLK))

    for axis in range(4):
        head[axis] = state[axis, SHARE : 2 * SHARE, :]

    density[...] = scaled

    def tail_row(row, carry):
        at = jnp.clip(filled - SHARE, 0, CAP - SHARE) + row
        for axis in range(3):
            tail[axis, pl.ds(row, 1), :] = pos_ref[axis, pl.ds(at, 1), :]
        tail[3, pl.ds(row, 1), :] = density[pl.ds(at, 1), :]
        return carry

    lax.fori_loop(0, SHARE, tail_row, 0, unroll=4)

    hood_z[FIELD_NULL : FIELD_NULL + 8, :] = jnp.zeros((8, BLK), jnp.float32)
    hood_t[FIELD_NULL : FIELD_NULL + 8, :] = jnp.zeros((8, BLK), jnp.float32)

    @pl.when(column == 0)
    def _():
        pl.semaphore_wait(barrier, 2 + 3 + 7 + 15 + 3)

    @pl.when(column > 0)
    def _():
        pl.semaphore_wait(barrier, 2 + 3 + 7 + 15 + 1)

    def remote(source, target, send, recv, device):
        return pltpu.make_async_remote_copy(
            src_ref=source, dst_ref=target, send_sem=send, recv_sem=recv, device_id=device, device_id_type=MESH
        )

    to_after = remote(tail, state.at[:, 0:SHARE, :], state_send.at[0], state_recv.at[0], (after, column))
    to_ahead = remote(head, state.at[:, SHARE + CAP : 2 * SHARE + CAP, :], state_send.at[1], state_recv.at[1], (ahead, column))
    to_after.start()
    to_ahead.start()
    list_copies = []
    for step in range(1, columns):
        other = lax.rem(column + step, columns)
        copy = remote(
            listed.at[pl.ds(pl.multiple_of(other * SHARE, SHARE), SHARE), :],
            listed_in.at[step - 1],
            list_send.at[step - 1],
            list_recv.at[step - 1],
            (piece, other),
        )
        copy.start()
        list_copies.append(copy)
    to_after.wait()
    to_ahead.wait()
    for copy in list_copies:
        copy.wait()
    mine = listed[pl.ds(pl.multiple_of(column * SHARE, SHARE), SHARE), :]
    for step in range(columns - 1):
        mine = mine + listed_in[step]
    listed_in[0] = mine

    lane = lax.broadcasted_iota(jnp.int32, (8, BLK), 1)
    sublane = lax.broadcasted_iota(jnp.int32, (8, BLK), 0)

    def to_row(block):
        return jnp.sum(block.T, axis=0, keepdims=True)

    def weights(at, group):
        rows = slice(8 * group, 8 * group + 8)
        dx = spread[0, rows, :] - at[0]
        dy = spread[1, rows, :] - at[1]
        dz = spread[2, rows, :] - at[2]
        squared = dx * dx + dy * dy + dz * dz
        near_by = jnp.maximum(1.0 - squared, 0.0)
        below = (squared + 0.01) * (spread[3, rows, :] + at[3])
        inverse = pl.reciprocal(below, approx=True)
        inverse = inverse * (2.0 - below * inverse)
        return near_by * near_by * inverse

    def source_rows(where_at):
        return [jnp.broadcast_to(state[axis, pl.ds(where_at, 1), :], (8, BLK)) for axis in range(4)]

    for degree, unit_first, units, tile_first in GROUPS:
        per_unit = 3 * degree

        def unit_body(index, carry, per_unit=per_unit, unit_first=unit_first, tile_first=tile_first):
            unit = unit_first + index
            spot = tab[UNIT_TAB + unit]
            row = SHARE + SHARE * column + spot
            for axis in range(4):
                one = jnp.broadcast_to(state[axis, pl.ds(row, 1), :], (BLK, BLK))
                spread[axis] = one.T
            base = tile_first + index * per_unit
            at = source_rows(tab[base])
            often = jnp.broadcast_to(listed_in[0, pl.ds(spot, 1), :], (8, BLK))
            sums = []
            for group in range(16):
                weight = weights(at, group) * often
                weight = jnp.where(sublane + 8 * group == lane, 0.0, weight)
                tiles[base, 8 * group : 8 * group + 8, :] = weight
                sums.append(weight)

            def tile_body(k, sums):
                at = source_rows(tab[base + k])
                new = []
                for group in range(16):
                    weight = weights(at, group)
                    tiles[base + k, 8 * group : 8 * group + 8, :] = weight
                    new.append(sums[group] + weight)
                return tuple(new)

            sums = lax.fori_loop(1, per_unit, tile_body, tuple(sums))
            rowbuf[pl.ds(unit, 1), :] = to_row(jnp.concatenate(sums, axis=0))
            return carry

        lax.fori_loop(0, units, unit_body, 0)

    def settle(target):
        for spot in range(SHARE):
            target[spot : spot + 1, :] = rowbuf[pl.ds(tab[SPOT_TAB + spot], 1), :]

    settle(diag)
    own_at = pl.multiple_of(SHARE * column, SHARE)
    rho = state[3, pl.ds(pl.multiple_of(SHARE + own_at, SHARE), SHARE), :]
    alive = lax.broadcasted_iota(jnp.int32, (SHARE, BLK), 0) + own_at < filled
    diagonal = 64.0 / rho + diag[...]
    diag[...] = diagonal
    source = jnp.where(alive, rhs_ref[...], 0.0)
    z = source / diagonal

    def exchange(own, hood, send, recv):
        source_ref = own

        def chunk(at):
            return hood.at[pl.ds(pl.multiple_of(at, SHARE), SHARE), :]

        here = 3 * SHARE + SHARE * column
        cases = []
        cases.append((column < columns - 1, here, (piece, column + 1), 0, 0))
        cases.append((column > 0, here, (piece, column - 1), 1, 1))
        for other in range(1, columns):
            cases.append((column == 0, 3 * SHARE + CAP, (ahead, other), 1 + other, 2))
        for other in range(1, columns):
            cases.append((column == other, SHARE * (other - 1), (after, 0), 2, 2 + other))
        return source_ref, chunk, here, cases

    def start_exchange(own, hood, send, recv):
        source_ref, chunk, here, cases = exchange(own, hood, send, recv)
        for when, at, device, send_at, recv_at in cases:
            @pl.when(when)
            def _(at=at, device=device, send_at=send_at, recv_at=recv_at):
                remote(source_ref, chunk(at), send.at[send_at], recv.at[recv_at], device).start()

    def finish_exchange(own, hood, send, recv):
        source_ref, chunk, here, cases = exchange(own, hood, send, recv)
        arrive = [
            (column > 0, here - SHARE, 0),
            (column < columns - 1, here + SHARE, 1),
            (column > 0, 3 * SHARE + CAP, 2),
        ]
        for other in range(1, columns):
            arrive.append((column == 0, SHARE * (other - 1), 2 + other))
        for when, at, recv_at in arrive:
            @pl.when(when)
            def _(at=at, recv_at=recv_at):
                remote(source_ref, chunk(at), send.at[0], recv.at[recv_at], (after, column)).wait_recv()

        for when, at, device, send_at, recv_at in cases:
            @pl.when(when)
            def _(at=at, device=device, send_at=send_at, recv_at=recv_at):
                remote(source_ref, chunk(at), send.at[send_at], recv.at[recv_at], device).wait_send()

    def product(value, own, hood, send, recv):
        own[...] = value
        start_exchange(own, hood, send, recv)
        hood[pl.ds(pl.multiple_of(3 * SHARE + own_at, SHARE), SHARE), :] = value

        def gather(ref, base, count):
            return [
                jnp.broadcast_to(ref[pl.ds(tab[FIELD_TAB + base + k], 1), :], (8, BLK)) for k in range(count)
            ]

        finish_exchange(own, hood, send, recv)

        for degree, unit_first, units, tile_first in GROUPS:
            def unit_body(index, carry, degree=degree, unit_first=unit_first, tile_first=tile_first):
                unit = unit_first + index
                base = tile_first + index * (3 * degree)
                fields = gather(hood, base, 3 * degree)
                sums = []
                for group in range(16):
                    rows = slice(8 * group, 8 * group + 8)
                    total = tiles[base, rows, :] * fields[0]
                    for k in range(1, 3 * degree):
                        total = total + tiles[base + k, rows, :] * fields[k]
                    sums.append(total)
                rowbuf[pl.ds(unit, 1), :] = to_row(jnp.concatenate(sums, axis=0))
                return carry

            lax.fori_loop(0, units, unit_body, 0)

    product(z, own_z, hood_z, z_send, z_recv)
    settle(y0)
    t = y0[...] / diag[...]
    product(t, own_t, hood_t, t_send, t_recv)
    settle(y1)

    z = own_z[...]
    t = own_t[...]
    source = jnp.where(alive, rhs_ref[...], 0.0)

    def partial(first, second):
        return jnp.sum(first * second, axis=0, keepdims=True)

    moments[0:1, :] = partial(source, z)
    moments[1:2, :] = partial(z, y0[...])
    moments[2:3, :] = partial(y0[...], t)
    moments[3:4, :] = partial(t, y1[...])
    moments[4:8, :] = jnp.zeros((4, BLK), jnp.float32)

    def share_sums(from_ref, stage, rank, size, member, send, recv):
        copies = []
        for step in range(1, size):
            copy = remote(
                from_ref, stage.at[rank], send.at[step - 1], recv.at[step - 1], member(lax.rem(rank + step, size))
            )
            copy.start()
            copies.append(copy)
        stage[rank] = from_ref[...]
        for copy in copies:
            copy.wait()
        total = stage[0]
        for k in range(1, size):
            total = total + stage[k]
        return total

    moments[8:16, :] = share_sums(moments.at[0:8, :], stage_a, rank_a, 8, member_a, a_send, a_recv)
    total = share_sums(moments.at[8:16, :], stage_b, chip, 16, member_b, b_send, b_recv)
    sums = jnp.sum(total, axis=1, keepdims=True)
    e0, e1, e2, e3 = (sums[k : k + 1, :] for k in range(4))
    f1 = e1 / e0
    f2 = e2 / e0
    f3 = e3 / e0
    lead = 1.0 / (1.0 - f1)
    spread_of = f2 - f1 * f1
    ratio = lead * lead * spread_of
    bent = f3 - 2.0 * f1 * f2 + f1 * f1 * f1
    second = spread_of / (spread_of - bent - lead * spread_of * spread_of)
    mix = ratio - lead * f1
    first_image = y0[...]
    direction = lead * t + mix * z
    x_ref[...] = lead * z + second * direction
    image = (lead - mix) * first_image + mix * source - lead * y1[...]
    r_ref[...] = lead * (first_image - f1 * source) - second * image


def body(positions, phase, neighbours, counts, phase_density, right_side):
    pieces = lax.axis_size("piece")
    columns = lax.axis_size("col")
    table = tables(counts, lax.axis_index("piece"), lax.axis_index("col"))
    vmem = pl.BlockSpec(memory_space=pltpu.VMEM)
    smem = pl.BlockSpec(memory_space=pltpu.SMEM)
    f32 = jnp.float32
    dma = pltpu.SemaphoreType.DMA
    shape = jax.ShapeDtypeStruct((SHARE, BLK), f32)
    return pl.pallas_call(
        functools.partial(kernel, pieces, columns),
        out_shape=(shape, shape),
        in_specs=[smem, smem, vmem, vmem, vmem, vmem],
        out_specs=(vmem, vmem),
        scratch_shapes=[
            pltpu.VMEM((4, STATE_NULL + 8, BLK), f32),
            pltpu.VMEM((4, BLK, BLK), f32),
            pltpu.VMEM((TILES, BLK, BLK), f32),
            pltpu.VMEM((CAP, BLK), f32),
            pltpu.VMEM((3, SHARE, BLK), f32),
            pltpu.VMEM((4, SHARE, BLK), f32),
            pltpu.VMEM((4, SHARE, BLK), f32),
            pltpu.VMEM((CAP, BLK), f32),
            pltpu.VMEM((SHARE, BLK), f32),
            pltpu.VMEM((SHARE, BLK), f32),
            pltpu.VMEM((FIELD_NULL + 8, BLK), f32),
            pltpu.VMEM((FIELD_NULL + 8, BLK), f32),
            pltpu.VMEM((UNITS, BLK), f32),
            pltpu.VMEM((SHARE, BLK), f32),
            pltpu.VMEM((SHARE, BLK), f32),
            pltpu.VMEM((SHARE, BLK), f32),
            pltpu.VMEM((16, BLK), f32),
            pltpu.VMEM((8, 8, BLK), f32),
            pltpu.VMEM((16, 8, BLK), f32),
            dma((2,)), dma((2,)), dma((3,)), dma((3,)),
            dma((5,)), dma((6,)), dma((5,)), dma((6,)),
            dma((7,)), dma((7,)), dma((15,)), dma((15,)),
        ],
        compiler_params=pltpu.CompilerParams(
            collective_id=0, has_side_effects=True, vmem_limit_bytes=60 * 1024 * 1024
        ),
        name="pressure",
    )(table, phase_density, positions, phase, neighbours, right_side)


def solution(mesh):
    placed = (
        P(None, "piece", None),
        P("piece", None),
        P("piece", "col"),
        P(),
        P(),
        P(("piece", "col"), None),
    )
    return jax.shard_map(
        body,
        mesh=mesh,
        in_specs=placed,
        out_specs=(P(("piece", "col"), None), P(("piece", "col"), None)),
        check_vma=False,
    )
```

time: 1120 us -> 97.3 us (0.09)
  matrix products: 488 us -> 0 us
  local copies, waits for them, and re-layouts: 236 us -> 5.96 us
  blocking collectives: 214 us -> 0 us
  Pallas kernels: 0 us -> 84.5 us
  waiting for transfers between devices: 71.8 us -> 0 us
  loops' own time: 47.6 us -> 0 us
  starting transfers between devices: 25.9 us -> 0 us
  between operations: 18 us -> 1.35 us
    dot_general x168 -> x0, matrix products: 488 us -> none  [pair_term(): jnp.einsum('gij,gj->gi', tile, remote, precision=lax.Precision.HIGHEST)]
    psum x3 -> x0, blocking collectives: 196 us -> none  [the longest x2 129 us: weighted_sum(): return lax.psum(inner(first, second), ('piece', 'col'))]
    gather x336 -> x0, local copies, waits for them, and re-layouts: 195 us -> none  [the longest x168 101 us: pair_term(): other = hood_state[:, where_at]]
    pallas_call x0 -> x1, Pallas kernels: none -> 84.5 us  [body(): pl.pallas_call(functools.partial(kernel, pieces, columns), out_shape=(sha...]
    reduce_scatter x3 -> x0, waiting for transfers between devices: 59.1 us -> none  [totals(): return lax.psum_scatter(part_sum, 'col', scatter_dimension=0, tiled=True)]
    another operation x3 -> x0, loops' own time: 47.6 us -> none  [own_terms(): output_blocks = lax.map(lambda start: group_sum(field_hood, start), starts)]
    ppermute x6 -> x0, starting transfers between devices: 25.8 us -> none  [the longest x3 19.6 us: padded(): lax.ppermute(tail, axis, [(i, (i + 1) % count) for i in range(ends)])]
    sub x24 -> x0, local copies, waits for them, and re-layouts: 18.2 us -> none  [pair_term(): own_pos[component][:, :, None] - other[component][:, None, :]]
  transfers between devices with their start and end apart: 9 -> 0, of which waited for: 7 -> 0; matrix products, arithmetic and copies ran while one was open for 0% -> 0% of each run, Pallas kernels for 0% -> 0%
where the time goes in v1:
time: 97.3 us; the launch traced here: 97 us
  Pallas kernels  84.5 us (87%)
  local copies, waits for them, and re-layouts  5.96 us (6%)
  other arithmetic  5.16 us (5%)
  between operations  1.35 us (1%)
    pallas_call x1, Pallas kernels, body(): pl.pallas_call(functools.partial(kernel, pieces, columns), out_shape=(sha...  84.5 us
    unnamed x25, local copies, waits for them, and re-layouts  4.65 us
    select_n x1, other arithmetic, tables(): field_at = jnp.where(good, field_at, FIELD_NULL)  2.51 us

profile of v1, /device:TPU:1, one launch (start us, length us, event | category | flops | bytes accessed | tf_op | source)
XLA Modules:
  0.0 97.0 jit_solution(287925021297758852)
XLA Ops:
  0.6 0.0 copy-start.7
  0.6 0.6 copy-done.7
  1.3 0.7 fusion.16
  2.0 0.0 copy-start.8
  2.0 0.0 copy-start.9
  2.0 0.0 copy-start.6
  2.6 0.0 copy-start.4
  2.6 0.0 copy-done.8
  2.6 0.0 copy-done.9
  2.7 0.0 copy-start.10
  2.7 0.0 copy-start.1
  2.7 0.0 copy-start
  2.7 0.6 copy-done.10
  3.3 0.1 select_reduce_fusion
  3.4 0.0 copy-start.5
  3.4 0.0 copy-done.6
  3.4 0.0 copy-done.4
  3.4 0.0 copy-done.1
  3.4 0.0 copy-done
  3.5 0.6 copy-done.5
  4.1 2.5 %select_select_fusion = (s32[600]{0:T(1024)S(1)}, s32[600]{0:T(1024)S(1)}) fusion(s32[]{:T(128)} %get-tuple-element.2, s32[]{:T(128)} %get-tuple-element.4, s32[]{:T(128)} %get-tuple-element.5, s32[600]{0:T(1024)S(1)} %copy-done, s32[600]{0:T(1024)S(1)} %copy-done.1, s32[]{:T(128)S(6)} %add.101, s32[]{:T(128)S(6)} %mul.21, s32[]{:T(128)} %get-tuple-element.3, ...), kind=kLoop, calls=%fused_computation.28 | loop fusion | flops 51000 | bytes 13224 | tf_op jit(solution)/shard_map/jit(_where)/select_n | solution.py:98
  6.6 1.9 %select_select_fusion.1 = s32[600]{0:T(1024)S(1)} fusion(s32[600]{0:T(1024)S(1)} %get-tuple-element.7, s32[]{:T(128)} %get-tuple-element.4, s32[]{:T(128)} %get-tuple-element.5, s32[600]{0:T(1024)S(1)} %copy-done, s32[600]{0:T(1024)S(1)} %copy-done.1, s32[]{:T(128)S(6)} %add.101, s32[]{:T(128)S(6)} %mul.21, s32[]{:T(128)} %get-tuple-element.3), kind=kLoop, calls=%fused_computation.29 | loop fusion | flops 15600 | bytes 9620 | tf_op jit(solution)/shard_map/jit(_where)/select_n | solution.py:92
  8.5 0.0 copy-start.3
  8.5 1.3 %concatenate.3.tab = s32[1265]{0:T(1024)} concatenate(s32[600]{0:T(1024)S(1)} %select_select_fusion.1, s32[600]{0:T(1024)S(1)} %get-tuple-element.6, s32[32]{0:T(128)S(1)} %get-tuple-element.9, s32[32]{0:T(128)S(1)} %fusion.13, s32[1]{0:T(128)} %bitcast), dimensions={0} | concatenate | bytes 10120 | tf_op jit(solution)/shard_map/concatenate | solution.py:106
  9.8 0.0 copy-done.3
  9.8 0.7 copy.16.near_ref
  10.5 84.5 %pressure.1 = (f32[32,128]{1,0:T(8,128)}, f32[32,128]{1,0:T(8,128)}) custom-call(s32[1265]{0:T(1024)} %concatenate.3.tab, f32[3]{0:T(128)} %dens.1, f32[3,128,128]{2,1,0:T(8,128)} %pos_ref.1, s32[128,128]{1,0:T(8,128)} %phase_ref.1, s32[128,7]{1,0:T(8,128)} %copy.16.near_ref, f32[32,128]{1,0:T(8,128)} %rhs_ref.1), custom_call_target="tpu_custom_call" | custom-call | tf_op jit(solution)/shard_map/pressure/pallas_call | solution.py:435
  95.0 0.0 copy-start.2
  95.0 1.3 %copy.19 = f32[32,128]{1,0:T(8,128)} copy(f32[32,128]{1,0:T(8,128)} %get-tuple-element.12) | data formatting | bytes 32768
  96.4 0.0 copy-done.2
  96.4 0.6 copy.20
  (2 shorter events, 0.0 us)
Async XLA Ops:
  0.6 0.7 copy-start.7
  2.0 0.7 copy-start.8
  2.0 0.7 copy-start.9
  2.0 1.4 %copy-start.6 = (pred[600]{0:T(1024)(128)(4,1)S(1)}, pred[600]{0:T(1024)(128)(4,1)}, u32[]{:S(2)}) copy-start(pred[600]{0:T(1024)(128)(4,1)} %constant.123) | copy-start | bytes 1804
  2.6 0.8 copy-start.4
  2.7 0.7 copy-start.10
  2.7 0.8 copy-start.1
  2.7 0.8 copy-start
  3.4 0.7 copy-start.5
  8.5 1.3 %copy-start.3 = (s32[128,7]{0,1:T(8,128)S(1)}, s32[128,7]{0,1:T(8,128)}, u32[]{:S(2)}) copy-start(s32[128,7]{0,1:T(8,128)} %param.15) | copy-start | bytes 10756
  95.0 1.3 %copy-start.2 = (f32[32,128]{1,0:T(8,128)S(1)}, f32[32,128]{1,0:T(8,128)}, u32[]{:S(2)}) copy-start(f32[32,128]{1,0:T(8,128)} %get-tuple-element.13) | copy-start | bytes 49156

commit v2 on v1

--- a/solution.py
+++ b/solution.py
@@ -2,7 +2,6 @@
 
 import jax
 import jax.numpy as jnp
-import numpy as np
 from jax import lax
 from jax.experimental import pallas as pl
 from jax.experimental.pallas import tpu as pltpu
@@ -13,10 +12,12 @@
 CAP = 128
 LAYER = 16
 SHARE = 32
-FAR = 1.0e4
-FAR_NULL = 2.0e4
+HOOD = 3 * SHARE
+FEATURES = 48
+FAR = 64.0
 STATE_NULL = 192
 FIELD_NULL = 256
+CELL_STEP = 10
 
 
 def layer_cells():
@@ -42,82 +43,31 @@
 CELLS = sorted(range(LAYER), key=lambda code: (len(NEAR[code]), code))
 
 
-def tile_plan():
-    rows, groups = [], []
-    own_cell, own_half = [], []
+def unit_plan():
+    groups, first_unit, first_tile = [], 0, 0
     for degree in (4, 6, 9):
-        cells = [code for code in CELLS if len(NEAR[code]) == degree]
-        groups.append((degree, len(own_cell), 2 * len(cells), len(rows)))
-        for code in cells:
-            for half in range(2):
-                own_cell.append(code)
-                own_half.append(half)
-                for kind in range(3):
-                    for other in NEAR[code]:
-                        rows.append((code, half, kind, other))
-    return np.array(rows, np.int32), groups, np.array(own_cell, np.int32), np.array(own_half, np.int32)
-
-
-ROWS, GROUPS, OWN_CELL, OWN_HALF = tile_plan()
-TILES = ROWS.shape[0]
-UNITS = 2 * LAYER
-RANK_OF = np.zeros((LAYER,), np.int32)
+        units = 2 * len([code for code in CELLS if len(NEAR[code]) == degree])
+        groups.append((degree, first_unit, units, first_tile))
+        first_unit += units
+        first_tile += 3 * degree * units
+    return groups, first_unit, first_tile
+
+
+GROUPS, UNITS, TILES = unit_plan()
+PATTERN = [0] * (LAYER * CELL_STEP)
+RANK_OF = [0] * LAYER
 for _rank, _code in enumerate(CELLS):
     RANK_OF[_code] = _rank
-
-
-def tables(counts, piece, column):
-    lanes = jnp.arange(counts.shape[0], dtype=jnp.int32)
-    start = jnp.sum(jnp.where(lanes < piece, counts, 0))
-    total = jnp.sum(counts)
-    filled = jnp.sum(jnp.where(lanes == piece, counts, 0))
-    before = jnp.sum(jnp.where(lanes == piece - 1, counts, 0))
-    first = start + SHARE * column
-
-    def local(cell, half):
-        return (cell - first) % LAYER + LAYER * half
-
-    cell, half, kind, other = (jnp.asarray(ROWS[:, i]) for i in range(4))
-    own = local(cell, half)
-    mate = local(other, half)
-    level = (first + own) // LAYER
-    lift = (first + mate) // LAYER - level
-    step = jnp.where(
-        kind == 0, lift, jnp.where(kind == 1, jnp.where(lift == -1, 0, -1), jnp.where(lift == 1, 0, 1))
-    )
-    order = LAYER * (level + step) + other
-    slot = order - start
-    good = (order >= 0) & (order < total) & (SHARE * column + own < filled)
-    state_at = jnp.where(slot < filled, SHARE + slot, SHARE + CAP + slot - filled)
-    state_at = jnp.where(good, state_at, STATE_NULL)
-    field_at = jnp.where(
-        slot < 0,
-        before + slot - SHARE,
-        jnp.where(slot < filled, 3 * SHARE + slot, 3 * SHARE + CAP + slot - filled),
-    )
-    field_at = jnp.where(good, field_at, FIELD_NULL)
-    units = local(jnp.asarray(OWN_CELL), jnp.asarray(OWN_HALF))
-    spots = jnp.arange(UNITS, dtype=jnp.int32)
-    cell_of = (first + spots) % LAYER
-    rank_of = jnp.sum(
-        jnp.where(cell_of[:, None] == jnp.arange(LAYER)[None], jnp.asarray(RANK_OF)[None], 0), axis=1
-    )
-    unit_of = 2 * rank_of + spots // LAYER
-    return jnp.concatenate([state_at, field_at, units, unit_of, filled[None]]).astype(jnp.int32)
-
-
-FIELD_TAB = TILES
-UNIT_TAB = 2 * TILES
-SPOT_TAB = 2 * TILES + UNITS
-FILLED_TAB = 2 * TILES + 2 * UNITS
+    PATTERN[_rank * CELL_STEP : _rank * CELL_STEP + len(NEAR[_code])] = NEAR[_code]
 
 
 def kernel(
     pieces, columns,
-    tab, dens, pos_ref, phase_ref, near_ref, rhs_ref,
+    counts, dens, pos_ref, phase_ref, near_ref, rhs_ref,
     x_ref, r_ref,
-    state, spread, tiles, listed, listed_in, head, tail, density,
-    own_z, own_t, hood_z, hood_t, rowbuf, diag, y0, y1, moments, stage_a, stage_b,
+    pattern, rank_of, state_at, field_at,
+    state, hood_state, right_rows, rho_rows, left_rows, right, left, tiles, listed, listed_in, head, tail, density,
+    own_z, own_t, hood_z, hood_t, near_field, rowbuf, diag, y0, y1, moments, stage_a, stage_b,
     state_send, state_recv, list_send, list_recv, z_send, z_recv, t_send, t_recv, a_send, a_recv, b_send, b_recv,
 ):
     piece = lax.axis_index("piece")
@@ -157,16 +107,25 @@
     def _():
         greet((after, 0))
 
-    filled = tab[FILLED_TAB]
-    slots = lax.broadcasted_iota(jnp.int32, (CAP, BLK), 0)
-    live = slots < filled
-    for axis in range(3):
-        state[axis, SHARE : SHARE + CAP, :] = jnp.where(live, pos_ref[axis], FAR)
-        state[axis, STATE_NULL : STATE_NULL + 8, :] = jnp.full((8, BLK), FAR_NULL, jnp.float32)
+    start, total, filled, before = 0, 0, 0, 0
+    for other in range(pieces):
+        count = counts[other]
+        start = start + jnp.where(other < piece, count, 0)
+        total = total + count
+        filled = filled + jnp.where(other == piece, count, 0)
+        before = before + jnp.where(other == piece - 1, count, 0)
+    first = start + SHARE * column
+    for place, code in enumerate(PATTERN):
+        pattern[place] = code
+    for code in range(LAYER):
+        rank_of[code] = RANK_OF[code]
+
     phase = phase_ref[...]
     scaled = jnp.where(phase == 0, dens[0], jnp.where(phase == 1, dens[1], dens[2])) * 64.0
-    state[3, SHARE : SHARE + CAP, :] = jnp.where(live, scaled, 64.0)
-    state[3, STATE_NULL : STATE_NULL + 8, :] = jnp.full((8, BLK), 64.0, jnp.float32)
+    density[...] = scaled
+    for axis in range(3):
+        state[axis, SHARE : SHARE + CAP, :] = pos_ref[axis]
+    state[3, SHARE : SHARE + CAP, :] = scaled
 
     near = near_ref[...]
     me_at = lax.broadcasted_iota(jnp.int32, near.shape, 0) + piece * CAP
@@ -189,6 +148,19 @@
 
     hood_z[FIELD_NULL : FIELD_NULL + 8, :] = jnp.zeros((8, BLK), jnp.float32)
     hood_t[FIELD_NULL : FIELD_NULL + 8, :] = jnp.zeros((8, BLK), jnp.float32)
+
+    def place_row(row, carry):
+        order = first + row - SHARE
+        slot = order - start
+        inside = (order >= 0) & (order < total)
+        at = jnp.where(slot < filled, SHARE + slot, SHARE + CAP + slot - filled)
+        state_at[row] = jnp.where(inside, jnp.clip(at, 0, STATE_NULL - 1), STATE_NULL)
+        at = jnp.where(slot < 0, before + slot - SHARE, 3 * SHARE + slot)
+        at = jnp.where(slot < filled, at, 3 * SHARE + CAP + slot - filled)
+        field_at[row] = jnp.where(inside, jnp.clip(at, 0, FIELD_NULL - 1), FIELD_NULL)
+        return carry
+
+    lax.fori_loop(0, HOOD, place_row, 0, unroll=2)
 
     @pl.when(column == 0)
     def _():
@@ -234,68 +206,135 @@
     def to_row(block):
         return jnp.sum(block.T, axis=0, keepdims=True)
 
-    def weights(at, group):
-        rows = slice(8 * group, 8 * group + 8)
-        dx = spread[0, rows, :] - at[0]
-        dy = spread[1, rows, :] - at[1]
-        dz = spread[2, rows, :] - at[2]
-        squared = dx * dx + dy * dy + dz * dz
-        near_by = jnp.maximum(1.0 - squared, 0.0)
-        below = (squared + 0.01) * (spread[3, rows, :] + at[3])
-        inverse = pl.reciprocal(below, approx=True)
-        inverse = inverse * (2.0 - below * inverse)
-        return near_by * near_by * inverse
-
-    def source_rows(where_at):
-        return [jnp.broadcast_to(state[axis, pl.ds(where_at, 1), :], (8, BLK)) for axis in range(4)]
+    origin_at = state_at[SHARE]
+    origins = [state[axis, pl.ds(origin_at, 1), :][:, 0:1] for axis in range(3)]
+    for axis in range(3):
+        state[axis, STATE_NULL : STATE_NULL + 8, :] = jnp.broadcast_to(origins[axis] + FAR, (8, BLK))
+    state[3, STATE_NULL : STATE_NULL + 8, :] = jnp.full((8, BLK), 64.0, jnp.float32)
+
+    def hood_row(row, carry):
+        for axis in range(4):
+            hood_state[axis, pl.ds(row, 1), :] = state[axis, pl.ds(state_at[row], 1), :]
+        return carry
+
+    lax.fori_loop(0, HOOD, hood_row, 0, unroll=8)
+
+    def parts(value, count):
+        out = []
+        for _ in range(count):
+            out.append(value.astype(jnp.bfloat16).astype(jnp.float32))
+            value = value - out[-1]
+        return out
+
+    def rows_at(row0, size):
+        rows = slice(row0, row0 + size)
+        coarse, middle, fine = [], [], []
+        for axis in range(3):
+            shifted = hood_state[axis, rows, :] - origins[axis]
+            big = jnp.floor(shifted * 16.0 + 0.5) * 0.0625
+            mid, low = parts(shifted - big, 2)
+            coarse.append(big)
+            middle.append(mid)
+            fine.append(low)
+        square = sum(big * big for big in coarse)
+        rest = sum(
+            (2.0 * big + (mid + low)) * (mid + low) for big, mid, low in zip(coarse, middle, fine)
+        )
+        return coarse, middle, fine, parts(square, 2), rest, parts(hood_state[3, rows, :], 3)
+
+    def put(target, size, row0, feature, value):
+        target[feature * size + row0 : feature * size + row0 + 8, :] = value
+
+    one = jnp.ones((8, BLK), jnp.float32)
+    zero = jnp.zeros((8, BLK), jnp.float32)
+    for row0 in range(0, HOOD, 8):
+        coarse, middle, fine, square, rest, rho = rows_at(row0, 8)
+        values = coarse + [one, one] + square + [zero]
+        values += middle + coarse + middle + fine + coarse + fine + middle
+        values += [one] * 3 + parts(rest, 3)
+        values += [zero] * (FEATURES - len(values))
+        for feature, value in enumerate(values):
+            put(right_rows, HOOD, row0, feature, value)
+        values = [zero] * 3 + [one] * 3 + rho + [zero] * 7
+        for feature, value in enumerate(values):
+            put(rho_rows, HOOD, row0, feature, value)
+        if SHARE <= row0 < 2 * SHARE:
+            c2, m2, f2 = ([-2.0 * value for value in group] for group in (coarse, middle, fine))
+            values = c2 + square + [one, one] + [zero]
+            values += c2 + m2 + m2 + c2 + f2 + m2 + f2
+            values += parts(rest + 0.01, 3) + [one] * 3
+            values += rho + [one] * 3
+            values += [zero] * (FEATURES - len(values))
+            for feature, value in enumerate(values):
+                put(left_rows, SHARE, row0 - SHARE, feature, value)
+
+    def pack_right(row, carry):
+        right[row, :, 0:BLK] = right_rows[pl.ds(row, FEATURES, stride=HOOD), :].astype(jnp.bfloat16)
+        right[row, 0:32, BLK : 2 * BLK] = jnp.zeros((32, BLK), jnp.bfloat16)
+        right[row, 32:48, BLK : 2 * BLK] = rho_rows[pl.ds(row, 16, stride=HOOD), :].astype(jnp.bfloat16)
+        return carry
+
+    lax.fori_loop(0, HOOD, pack_right, 0, unroll=4)
+
+    def pack_left(row, carry):
+        left[row] = left_rows[pl.ds(row, FEATURES, stride=SHARE), :].T.astype(jnp.bfloat16)
+        return carry
+
+    lax.fori_loop(0, SHARE, pack_left, 0, unroll=4)
+
+    def unit_at(unit):
+        rank = unit // 2
+        cell = pattern[rank * CELL_STEP]
+        own = ((cell - first) & (LAYER - 1)) + LAYER * lax.rem(unit, 2)
+        base = ((first + own) & ~(LAYER - 1)) - first + SHARE
+        return rank * CELL_STEP, own, base
+
+    def sources(place, base, degree):
+        return [
+            base + step * LAYER + pattern[place + k] for step in (0, -1, 1) for k in range(degree)
+        ]
 
     for degree, unit_first, units, tile_first in GROUPS:
-        per_unit = 3 * degree
-
-        def unit_body(index, carry, per_unit=per_unit, unit_first=unit_first, tile_first=tile_first):
+
+        def weigh_body(index, carry, degree=degree, unit_first=unit_first, tile_first=tile_first):
             unit = unit_first + index
-            spot = tab[UNIT_TAB + unit]
-            row = SHARE + SHARE * column + spot
-            for axis in range(4):
-                one = jnp.broadcast_to(state[axis, pl.ds(row, 1), :], (BLK, BLK))
-                spread[axis] = one.T
-            base = tile_first + index * per_unit
-            at = source_rows(tab[base])
-            often = jnp.broadcast_to(listed_in[0, pl.ds(spot, 1), :], (8, BLK))
-            sums = []
-            for group in range(16):
-                weight = weights(at, group) * often
-                weight = jnp.where(sublane + 8 * group == lane, 0.0, weight)
-                tiles[base, 8 * group : 8 * group + 8, :] = weight
-                sums.append(weight)
-
-            def tile_body(k, sums):
-                at = source_rows(tab[base + k])
-                new = []
+            place, own, base = unit_at(unit)
+            mine = left[own]
+            tile = tile_first + index * (3 * degree)
+            often = jnp.broadcast_to(listed_in[0, pl.ds(own, 1), :], (8, BLK))
+            sums = [None] * 16
+            for k, at in enumerate(sources(place, base, degree)):
+                both = jnp.dot(mine, right[at], preferred_element_type=jnp.float32)
                 for group in range(16):
-                    weight = weights(at, group)
-                    tiles[base + k, 8 * group : 8 * group + 8, :] = weight
-                    new.append(sums[group] + weight)
-                return tuple(new)
-
-            sums = lax.fori_loop(1, per_unit, tile_body, tuple(sums))
+                    rows = slice(8 * group, 8 * group + 8)
+                    apart = both[rows, 0:BLK]
+                    near_by = jnp.maximum(1.01 - apart, 0.0)
+                    weight = near_by * near_by * (1.0 / (apart * both[rows, BLK : 2 * BLK]))
+                    if k == 0:
+                        weight = jnp.where(sublane + 8 * group == lane, 0.0, weight * often)
+                        sums[group] = weight
+                    else:
+                        sums[group] = sums[group] + weight
+                    tiles[tile + k, rows, :] = weight
             rowbuf[pl.ds(unit, 1), :] = to_row(jnp.concatenate(sums, axis=0))
             return carry
 
-        lax.fori_loop(0, units, unit_body, 0)
-
-    def settle(target):
-        for spot in range(SHARE):
-            target[spot : spot + 1, :] = rowbuf[pl.ds(tab[SPOT_TAB + spot], 1), :]
-
-    settle(diag)
+        lax.fori_loop(0, units, weigh_body, 0)
+
+    spots = []
+    for spot in range(SHARE):
+        rank = rank_of[(first + spot) & (LAYER - 1)]
+        spots.append(2 * rank + spot // LAYER)
+
+    def settle():
+        return jnp.concatenate([rowbuf[pl.ds(spot, 1), :] for spot in spots], axis=0)
+
     own_at = pl.multiple_of(SHARE * column, SHARE)
-    rho = state[3, pl.ds(pl.multiple_of(SHARE + own_at, SHARE), SHARE), :]
     alive = lax.broadcasted_iota(jnp.int32, (SHARE, BLK), 0) + own_at < filled
-    diagonal = 64.0 / rho + diag[...]
+    diagonal = 64.0 / hood_state[3, SHARE : 2 * SHARE, :] + settle()
     diag[...] = diagonal
     source = jnp.where(alive, rhs_ref[...], 0.0)
-    z = source / diagonal
+    z = jnp.where(alive, source / diagonal, 0.0)
 
     def exchange(own, hood, send, recv):
         source_ref = own
@@ -344,35 +383,40 @@
         start_exchange(own, hood, send, recv)
         hood[pl.ds(pl.multiple_of(3 * SHARE + own_at, SHARE), SHARE), :] = value
 
-        def gather(ref, base, count):
-            return [
-                jnp.broadcast_to(ref[pl.ds(tab[FIELD_TAB + base + k], 1), :], (8, BLK)) for k in range(count)
-            ]
-
         finish_exchange(own, hood, send, recv)
 
+        def field_row(row, carry):
+            near_field[pl.ds(row, 1), :] = hood[pl.ds(field_at[row], 1), :]
+            return carry
+
+        lax.fori_loop(0, HOOD, field_row, 0, unroll=8)
+
         for degree, unit_first, units, tile_first in GROUPS:
+
             def unit_body(index, carry, degree=degree, unit_first=unit_first, tile_first=tile_first):
                 unit = unit_first + index
-                base = tile_first + index * (3 * degree)
-                fields = gather(hood, base, 3 * degree)
+                place, own_spot, base = unit_at(unit)
+                tile = tile_first + index * (3 * degree)
+                fields = [
+                    jnp.broadcast_to(near_field[pl.ds(at, 1), :], (8, BLK)) for at in sources(place, base, degree)
+                ]
                 sums = []
                 for group in range(16):
                     rows = slice(8 * group, 8 * group + 8)
-                    total = tiles[base, rows, :] * fields[0]
+                    total = tiles[tile, rows, :] * fields[0]
                     for k in range(1, 3 * degree):
-                        total = total + tiles[base + k, rows, :] * fields[k]
+                        total = total + tiles[tile + k, rows, :] * fields[k]
                     sums.append(total)
                 rowbuf[pl.ds(unit, 1), :] = to_row(jnp.concatenate(sums, axis=0))
                 return carry
 
-            lax.fori_loop(0, units, unit_body, 0)
+            lax.fori_loop(0, units, unit_body, 0, unroll=2)
 
     product(z, own_z, hood_z, z_send, z_recv)
-    settle(y0)
-    t = y0[...] / diag[...]
+    y0[...] = jnp.where(alive, settle(), 0.0)
+    t = jnp.where(alive, y0[...] / diag[...], 0.0)
     product(t, own_t, hood_t, t_send, t_recv)
-    settle(y1)
+    y1[...] = jnp.where(alive, settle(), 0.0)
 
     z = own_z[...]
     t = own_t[...]
@@ -426,7 +470,6 @@
 def body(positions, phase, neighbours, counts, phase_density, right_side):
     pieces = lax.axis_size("piece")
     columns = lax.axis_size("col")
-    table = tables(counts, lax.axis_index("piece"), lax.axis_index("col"))
     vmem = pl.BlockSpec(memory_space=pltpu.VMEM)
     smem = pl.BlockSpec(memory_space=pltpu.SMEM)
     f32 = jnp.float32
@@ -438,8 +481,17 @@
         in_specs=[smem, smem, vmem, vmem, vmem, vmem],
         out_specs=(vmem, vmem),
         scratch_shapes=[
+            pltpu.SMEM((LAYER * CELL_STEP,), jnp.int32),
+            pltpu.SMEM((LAYER,), jnp.int32),
+            pltpu.SMEM((HOOD,), jnp.int32),
+            pltpu.SMEM((HOOD,), jnp.int32),
             pltpu.VMEM((4, STATE_NULL + 8, BLK), f32),
-            pltpu.VMEM((4, BLK, BLK), f32),
+            pltpu.VMEM((4, HOOD, BLK), f32),
+            pltpu.VMEM((FEATURES * HOOD, BLK), f32),
+            pltpu.VMEM((16 * HOOD, BLK), f32),
+            pltpu.VMEM((FEATURES * SHARE, BLK), f32),
+            pltpu.VMEM((HOOD, FEATURES, 2 * BLK), jnp.bfloat16),
+            pltpu.VMEM((SHARE, BLK, FEATURES), jnp.bfloat16),
             pltpu.VMEM((TILES, BLK, BLK), f32),
             pltpu.VMEM((CAP, BLK), f32),
             pltpu.VMEM((3, SHARE, BLK), f32),
@@ -450,6 +502,7 @@
             pltpu.VMEM((SHARE, BLK), f32),
             pltpu.VMEM((FIELD_NULL + 8, BLK), f32),
             pltpu.VMEM((FIELD_NULL + 8, BLK), f32),
+            pltpu.VMEM((HOOD, BLK), f32),
             pltpu.VMEM((UNITS, BLK), f32),
             pltpu.VMEM((SHARE, BLK), f32),
             pltpu.VMEM((SHARE, BLK), f32),
@@ -465,7 +518,7 @@
             collective_id=0, has_side_effects=True, vmem_limit_bytes=60 * 1024 * 1024
         ),
         name="pressure",
-    )(table, phase_density, positions, phase, neighbours, right_side)
+    )(counts, phase_density, positions, phase, neighbours, right_side)
 
 
 def solution(mesh):

time: 97.3 us -> 69 us (0.71)
  Pallas kernels: 84.5 us -> 64.8 us
  other arithmetic: 5.16 us -> 0 us
  local copies, waits for them, and re-layouts: 5.96 us -> 3.34 us
    pallas_call x1, Pallas kernels: 84.5 us -> 64.8 us  [body(): pl.pallas_call(functools.partial(kernel, pieces, columns), out_shape=(sha...]
    select_n x3 -> x0, other arithmetic: 4.38 us -> none  [the longest x1 2.51 us: tables(): field_at = jnp.where(good, field_at, FIELD_NULL)]
    concatenate x1 -> x0, local copies, waits for them, and re-layouts: 1.31 us -> none  [tables(): jnp.concatenate([state_at, field_at, units, unit_of, filled[None]])]
    unnamed x25 -> x5, local copies, waits for them, and re-layouts: 4.65 us -> 3.34 us
where the time goes in v2:
time: 69 us; the launch traced here: 68.8 us
  Pallas kernels  64.8 us (94%)
  local copies, waits for them, and re-layouts  3.34 us (5%)
    pallas_call x1, Pallas kernels, body(): pl.pallas_call(functools.partial(kernel, pieces, columns), out_shape=(sha...  64.8 us
    unnamed x5, local copies, waits for them, and re-layouts  3.34 us

profile of v2, /device:TPU:1, one launch (start us, length us, event | category | flops | bytes accessed | tf_op | source)
XLA Modules:
  0.0 68.8 jit_solution(13914801985262363579)
XLA Ops:
  0.6 1.4 %copy.8.near_ref = s32[128,7]{1,0:T(8,128)} copy(s32[128,7]{0,1:T(8,128)} %param.8) | data formatting | bytes 7168 | tf_op args[2]
  2.0 64.8 %pressure.1 = (f32[32,128]{1,0:T(8,128)}, f32[32,128]{1,0:T(8,128)}) custom-call(s32[32]{0:T(128)} %counts.1, f32[3]{0:T(128)} %dens.1, f32[3,128,128]{2,1,0:T(8,128)} %pos_ref.1, s32[128,128]{1,0:T(8,128)} %phase_ref.1, s32[128,7]{1,0:T(8,128)} %copy.8.near_ref, f32[32,128]{1,0:T(8,128)} %rhs_ref.1), custom_call_target="tpu_custom_call" | custom-call | tf_op jit(solution)/shard_map/pressure/pallas_call | solution.py:478
  66.8 0.0 copy-start
  66.8 1.3 %copy.11 = f32[32,128]{1,0:T(8,128)} copy(f32[32,128]{1,0:T(8,128)} %get-tuple-element.4) | data formatting | bytes 32768
  68.2 0.0 copy-done
  68.2 0.6 copy.12
Async XLA Ops:
  66.8 1.3 %copy-start = (f32[32,128]{1,0:T(8,128)S(1)}, f32[32,128]{1,0:T(8,128)}, u32[]{:S(2)}) copy-start(f32[32,128]{1,0:T(8,128)} %get-tuple-element.5) | copy-start | bytes 49156

commit v3 on v2

v3 whole, which is shorter than its diff:
```python
import functools

import jax
import jax.numpy as jnp
from jax import lax
from jax.experimental import pallas as pl
from jax.experimental.pallas import tpu as pltpu
from jax.sharding import PartitionSpec as P

MESH = pl.DeviceIdType.MESH
BLK = 128
CAP = 128
LAYER = 16
SHARE = 32
HOOD = 3 * SHARE
FEATURES = 48
FAR = 64.0
STATE_NULL = 192
FIELD_NULL = 256
CELL_STEP = 10


def layer_cells():
    place = []
    for code in range(LAYER):
        across = code % 2 + 2 * (code // 4 % 2)
        along = code // 2 % 2 + 2 * (code // 8 % 2)
        place.append((across, along))
    near = []
    for code in range(LAYER):
        others = [
            other
            for other in range(LAYER)
            if other != code
            and abs(place[other][0] - place[code][0]) <= 1
            and abs(place[other][1] - place[code][1]) <= 1
        ]
        near.append([code] + others)
    return near


NEAR = layer_cells()
CELLS = sorted(range(LAYER), key=lambda code: (len(NEAR[code]), code))


def unit_plan():
    groups, first_unit, first_tile = [], 0, 0
    for degree in (4, 6, 9):
        units = 2 * len([code for code in CELLS if len(NEAR[code]) == degree])
        groups.append((degree, first_unit, units, first_tile))
        first_unit += units
        first_tile += 3 * degree * units
    return groups, first_unit, first_tile


GROUPS, UNITS, TILES = unit_plan()
PATTERN = [0] * (LAYER * CELL_STEP)
RANK_OF = [0] * LAYER
for _rank, _code in enumerate(CELLS):
    RANK_OF[_code] = _rank
    PATTERN[_rank * CELL_STEP : _rank * CELL_STEP + len(NEAR[_code])] = NEAR[_code]


def kernel(
    pieces, columns,
    counts, dens, pos_ref, phase_ref, near_ref, rhs_ref,
    x_ref, r_ref,
    pattern, rank_of, state_at, field_at,
    state, hood_state, right_rows, rho_rows, left_rows, right, left, tiles, accs,
    hits, hits_in, often, rhs_all, head, tail, density,
    own_z, own_t, hood_z, hood_t, near_field, rowbuf, diag, y0, y1, source_at, final, first_field, moments, stage_a, stage_b,
    state_send, state_recv, hits_send, hits_recv, rhs_send, rhs_recv, z_send, z_recv, t_send, t_recv, a_send, a_recv, b_send, b_recv,
):
    piece = lax.axis_index("piece")
    column = lax.axis_index("col")
    after = lax.rem(piece + 1, pieces)
    ahead = lax.rem(piece + pieces - 1, pieces)
    core = lax.rem(piece, 2)
    chip = piece // 2
    rank_a = column * 2 + core

    def member_a(rank):
        return (chip * 2 + lax.rem(rank, 2), rank // 2)

    def member_b(rank):
        return (rank * 2 + core, column)

    barrier = pltpu.get_barrier_semaphore()

    def greet(target):
        pl.semaphore_signal(barrier, inc=1, device_id=target, device_id_type=MESH)

    greet((after, column))
    greet((ahead, column))
    for step in range(1, columns):
        greet((piece, lax.rem(column + step, columns)))
    for step in range(1, 8):
        greet(member_a(lax.rem(rank_a + step, 8)))
    for step in range(1, 16):
        greet(member_b(lax.rem(chip + step, 16)))

    @pl.when(column == 0)
    def _():
        for other in range(1, columns):
            greet((ahead, other))

    @pl.when(column > 0)
    def _():
        greet((after, 0))

    start, total, filled, before = 0, 0, 0, 0
    for other in range(pieces):
        count = counts[other]
        start = start + jnp.where(other < piece, count, 0)
        total = total + count
        filled = filled + jnp.where(other == piece, count, 0)
        before = before + jnp.where(other == piece - 1, count, 0)
    own_first = SHARE * column
    frame = jnp.clip(jnp.minimum(own_first, filled - SHARE), 0, CAP - SHARE)
    first = start + frame
    for place, code in enumerate(PATTERN):
        pattern[place] = code
    for code in range(LAYER):
        rank_of[code] = RANK_OF[code]

    phase = phase_ref[...]
    scaled = jnp.where(phase == 0, dens[0], jnp.where(phase == 1, dens[1], dens[2])) * 64.0
    density[...] = scaled
    for axis in range(3):
        state[axis, SHARE : SHARE + CAP, :] = pos_ref[axis]
    state[3, SHARE : SHARE + CAP, :] = scaled

    near = near_ref[...]
    me_at = lax.broadcasted_iota(jnp.int32, near.shape, 1) + piece * CAP
    hits[0:1, :] = jnp.sum(jnp.where(near == me_at, 1.0, 0.0), axis=0, keepdims=True)

    for axis in range(4):
        head[axis] = pos_ref[axis, 0:SHARE, :] if axis < 3 else scaled[0:SHARE, :]

    density[...] = scaled

    def tail_row(row, carry):
        at = jnp.clip(filled - SHARE, 0, CAP - SHARE) + row
        for axis in range(3):
            tail[axis, pl.ds(row, 1), :] = pos_ref[axis, pl.ds(at, 1), :]
        tail[3, pl.ds(row, 1), :] = density[pl.ds(at, 1), :]
        return carry

    lax.fori_loop(0, SHARE, tail_row, 0, unroll=4)

    hood_z[FIELD_NULL : FIELD_NULL + 8, :] = jnp.zeros((8, BLK), jnp.float32)
    hood_t[FIELD_NULL : FIELD_NULL + 8, :] = jnp.zeros((8, BLK), jnp.float32)

    def place_row(row, carry):
        order = first + row - SHARE
        slot = order - start
        inside = (order >= 0) & (order < total)
        at = jnp.where(slot < filled, SHARE + slot, SHARE + CAP + slot - filled)
        state_at[row] = jnp.where(inside, jnp.clip(at, 0, STATE_NULL - 1), STATE_NULL)
        at = jnp.where(slot < 0, before + slot - SHARE, 3 * SHARE + slot)
        at = jnp.where(slot < filled, at, 3 * SHARE + CAP + slot - filled)
        field_at[row] = jnp.where(inside, jnp.clip(at, 0, FIELD_NULL - 1), FIELD_NULL)
        return carry

    lax.fori_loop(0, HOOD, place_row, 0, unroll=2)

    lane = lax.broadcasted_iota(jnp.int32, (8, BLK), 1)
    sublane = lax.broadcasted_iota(jnp.int32, (8, BLK), 0)

    def to_row(block):
        return jnp.sum(block.T, axis=0, keepdims=True)

    def frame_row(row, carry):
        for axis in range(3):
            hood_state[axis, pl.ds(SHARE + row, 1), :] = pos_ref[axis, pl.ds(frame + row, 1), :]
        hood_state[3, pl.ds(SHARE + row, 1), :] = density[pl.ds(frame + row, 1), :]
        return carry

    lax.fori_loop(0, SHARE, frame_row, 0, unroll=8)
    origins = [hood_state[axis, SHARE : SHARE + 1, 0:1] for axis in range(3)]

    def parts(value, count):
        out = []
        for _ in range(count):
            out.append(value.astype(jnp.bfloat16).astype(jnp.float32))
            value = value - out[-1]
        return out

    def rows_at(row0, size):
        rows = slice(row0, row0 + size)
        coarse, middle, fine = [], [], []
        for axis in range(3):
            shifted = hood_state[axis, rows, :] - origins[axis]
            big = jnp.floor(shifted * 16.0 + 0.5) * 0.0625
            mid, low = parts(shifted - big, 2)
            coarse.append(big)
            middle.append(mid)
            fine.append(low)
        square = sum(big * big for big in coarse)
        rest = sum(
            (2.0 * big + (mid + low)) * (mid + low) for big, mid, low in zip(coarse, middle, fine)
        )
        return coarse, middle, fine, parts(square, 2), rest, parts(hood_state[3, rows, :], 3)

    one = jnp.ones((8, BLK), jnp.float32)
    zero = jnp.zeros((8, BLK), jnp.float32)

    def put(target, count, row0, values):
        for feature in range(count):
            at = (row0 // 8 * count + feature) * 8
            target[at : at + 8, :] = values[feature] if feature < len(values) else zero

    def build_rows(starts):
        for row0 in starts:
            coarse, middle, fine, square, rest, rho = rows_at(row0, 8)
            values = coarse + [one, one] + square + [zero]
            values += middle + coarse + middle + fine + coarse + fine + middle
            values += [one] * 3 + parts(rest, 3)
            put(right_rows, FEATURES, row0, values)
            put(rho_rows, 16, row0, [zero] * 3 + [one] * 3 + rho)
            if SHARE <= row0 < 2 * SHARE:
                c2, m2, f2 = ([-2.0 * value for value in group] for group in (coarse, middle, fine))
                values = c2 + square + [one, one] + [zero]
                values += c2 + m2 + m2 + c2 + f2 + m2 + f2
                values += parts(rest + 0.01, 3) + [one] * 3
                values += rho + [one] * 3
                put(left_rows, FEATURES, row0 - SHARE, values)

    def pack_right(row, carry):
        group, inner = row // 8, lax.rem(row, 8)
        right[row, :, 0:BLK] = right_rows[pl.ds(group * (8 * FEATURES) + inner, FEATURES, stride=8), :].astype(jnp.bfloat16)
        right[row, 0:32, BLK : 2 * BLK] = jnp.zeros((32, BLK), jnp.bfloat16)
        right[row, 32:48, BLK : 2 * BLK] = rho_rows[pl.ds(group * 128 + inner, 16, stride=8), :].astype(jnp.bfloat16)
        return carry

    def pack_left(row, carry):
        group, inner = row // 8, lax.rem(row, 8)
        left[row] = left_rows[pl.ds(group * (8 * FEATURES) + inner, FEATURES, stride=8), :].T.astype(jnp.bfloat16)
        return carry

    build_rows(range(SHARE, 2 * SHARE, 8))
    lax.fori_loop(SHARE, 2 * SHARE, pack_right, 0, unroll=4)
    lax.fori_loop(0, SHARE, pack_left, 0, unroll=4)

    def unit_at(unit):
        rank = unit // 2
        place = rank * CELL_STEP
        half = LAYER * lax.rem(unit, 2)
        own = ((pattern[place] - first) & (LAYER - 1)) + half
        base = ((first + own) & ~(LAYER - 1)) - first + SHARE
        return place, half, own, base

    def mates(place, half, degree):
        return [((pattern[place + k] - first) & (LAYER - 1)) + half + SHARE for k in range(degree)]

    def others(place, half, base, degree):
        lower, upper = [], []
        for k, mate in enumerate(mates(place, half, degree)):
            level = base + pattern[place + k]
            lower.append(level - jnp.where(mate < level, 0, LAYER))
            upper.append(level + jnp.where(mate > level, 0, LAYER))
        return lower + upper

    def weigh(mine, at, tile, sums, multiply):
        both = jnp.dot(mine, right[at], preferred_element_type=jnp.float32)
        out = []
        for group in range(16):
            rows = slice(8 * group, 8 * group + 8)
            apart = both[rows, 0:BLK]
            near_by = jnp.maximum(1.01 - apart, 0.0)
            weight = near_by * near_by * (1.0 / (apart * both[rows, BLK : 2 * BLK]))
            if multiply is not None:
                weight = jnp.where(sublane + 8 * group == lane, 0.0, weight * multiply)
            tiles[tile, rows, :] = weight
            out.append(weight if sums is None else sums[group] + weight)
        return out

    @pl.when(column == 0)
    def _():
        pl.semaphore_wait(barrier, 2 + 3 + 7 + 15 + 3)

    @pl.when(column > 0)
    def _():
        pl.semaphore_wait(barrier, 2 + 3 + 7 + 15 + 1)

    def remote(source, target, send, recv, device):
        return pltpu.make_async_remote_copy(
            src_ref=source, dst_ref=target, send_sem=send, recv_sem=recv, device_id=device, device_id_type=MESH
        )

    to_after = remote(tail, state.at[:, 0:SHARE, :], state_send.at[0], state_recv.at[0], (after, column))
    to_ahead = remote(head, state.at[:, SHARE + CAP : 2 * SHARE + CAP, :], state_send.at[1], state_recv.at[1], (ahead, column))
    to_after.start()
    to_ahead.start()
    early = [to_after, to_ahead]
    own_at = pl.multiple_of(own_first, SHARE)
    for step in range(1, columns):
        other = lax.rem(column + step, columns)
        early.append(
            remote(hits.at[0:1, :], hits_in.at[step - 1, 0:1, :], hits_send.at[step - 1], hits_recv.at[step - 1], (piece, other))
        )
        early.append(
            remote(rhs_ref, rhs_all.at[pl.ds(own_at, SHARE), :], rhs_send.at[step - 1], rhs_recv.at[step - 1], (piece, other))
        )
    for copy in early[2:]:
        copy.start()
    rhs_all[pl.ds(own_at, SHARE), :] = rhs_ref[...]

    for degree, unit_first, units, tile_first in GROUPS:

        def near_body(index, carry, degree=degree, unit_first=unit_first, tile_first=tile_first):
            unit = unit_first + index
            place, half, own, base = unit_at(unit)
            mine = left[own]
            tile = tile_first + index * (3 * degree)
            sums = None
            for k, at in enumerate(mates(place, half, degree)):
                if k > 0:
                    sums = weigh(mine, at, tile + k, sums, None)
            for group in range(16):
                accs[unit, 8 * group : 8 * group + 8, :] = sums[group]
            return carry

        lax.fori_loop(0, units, near_body, 0, unroll=2 if degree < 9 else 1)

    for copy in early:
        copy.wait()
    total_hits = hits[0:1, :]
    for step in range(columns - 1):
        total_hits = total_hits + hits_in[step, 0:1, :]
    often[...] = jnp.broadcast_to(total_hits, (CAP, BLK)).T

    for axis in range(3):
        state[axis, STATE_NULL : STATE_NULL + 8, :] = jnp.broadcast_to(origins[axis] + FAR, (8, BLK))
    state[3, STATE_NULL : STATE_NULL + 8, :] = jnp.full((8, BLK), 64.0, jnp.float32)

    def hood_row(index, carry):
        row = index + SHARE * (index // SHARE)
        for axis in range(4):
            hood_state[axis, pl.ds(row, 1), :] = state[axis, pl.ds(state_at[row], 1), :]
        return carry

    lax.fori_loop(0, 2 * SHARE, hood_row, 0, unroll=8)
    build_rows([row for row in range(0, HOOD, 8) if not SHARE <= row < 2 * SHARE])
    lax.fori_loop(0, SHARE, pack_right, 0, unroll=4)
    lax.fori_loop(2 * SHARE, HOOD, pack_right, 0, unroll=4)

    for degree, unit_first, units, tile_first in GROUPS:

        def far_body(index, carry, degree=degree, unit_first=unit_first, tile_first=tile_first):
            unit = unit_first + index
            place, half, own, base = unit_at(unit)
            mine = left[own]
            tile = tile_first + index * (3 * degree)
            listed = jnp.broadcast_to(often[pl.ds(frame + own, 1), :], (8, BLK))
            sums = [accs[unit, 8 * group : 8 * group + 8, :] for group in range(16)]
            sums = weigh(mine, SHARE + own, tile, sums, listed)
            for k, at in enumerate(others(place, half, base, degree)):
                sums = weigh(mine, at, tile + degree + k, sums, None)
            rowbuf[pl.ds(unit, 1), :] = to_row(jnp.concatenate(sums, axis=0))
            return carry

        lax.fori_loop(0, units, far_body, 0)


    spots = []
    for spot in range(SHARE):
        rank = rank_of[(first + spot) & (LAYER - 1)]
        spots.append(2 * rank + spot // LAYER)

    def settle():
        return jnp.concatenate([rowbuf[pl.ds(spot, 1), :] for spot in spots], axis=0)

    spot_at = lax.broadcasted_iota(jnp.int32, (SHARE, BLK), 0)
    mine_here = (spot_at + frame >= own_first) & (spot_at + frame < own_first + SHARE)
    diag[...] = 64.0 / hood_state[3, SHARE : 2 * SHARE, :] + settle()
    for spot in range(SHARE):
        source_at[spot : spot + 1, :] = rhs_all[pl.ds(frame + spot, 1), :]

    own_live = spot_at + own_first < filled

    def to_own(ref):
        places = [jnp.clip(own_first + spot - frame, 0, SHARE - 1) for spot in range(SHARE)]
        rows = jnp.concatenate([ref[pl.ds(place, 1), :] for place in places], axis=0)
        return jnp.where(own_live, rows, 0.0)

    def exchange(own, hood, send, recv):
        source_ref = own

        def chunk(at):
            return hood.at[pl.ds(pl.multiple_of(at, SHARE), SHARE), :]

        here = 3 * SHARE + SHARE * column
        cases = []
        cases.append((column < columns - 1, here, (piece, column + 1), 0, 0))
        cases.append((column > 0, here, (piece, column - 1), 1, 1))
        cases.append((column < columns - 2, here, (piece, column + 2), 5, 6))
        for other in range(1, columns):
            cases.append((column == 0, 3 * SHARE + CAP, (ahead, other), 1 + other, 2))
        for other in range(1, columns):
            cases.append((column == other, SHARE * (other - 1), (after, 0), 2, 2 + other))
        return source_ref, chunk, here, cases

    def start_exchange(own, hood, send, recv):
        source_ref, chunk, here, cases = exchange(own, hood, send, recv)
        for when, at, device, send_at, recv_at in cases:
            @pl.when(when)
            def _(at=at, device=device, send_at=send_at, recv_at=recv_at):
                remote(source_ref, chunk(at), send.at[send_at], recv.at[recv_at], device).start()

    def finish_exchange(own, hood, send, recv):
        source_ref, chunk, here, cases = exchange(own, hood, send, recv)
        arrive = [
            (column > 0, here - SHARE, 0),
            (column < columns - 1, here + SHARE, 1),
            (column > 0, 3 * SHARE + CAP, 2),
            (column > 1, here - 2 * SHARE, 6),
        ]
        for other in range(1, columns):
            arrive.append((column == 0, SHARE * (other - 1), 2 + other))
        for when, at, recv_at in arrive:
            @pl.when(when)
            def _(at=at, recv_at=recv_at):
                remote(source_ref, chunk(at), send.at[0], recv.at[recv_at], (after, column)).wait_recv()

        for when, at, device, send_at, recv_at in cases:
            @pl.when(when)
            def _(at=at, device=device, send_at=send_at, recv_at=recv_at):
                remote(source_ref, chunk(at), send.at[send_at], recv.at[recv_at], device).wait_send()

    def product(value, own, hood, send, recv):
        near_field[SHARE : 2 * SHARE, :] = value
        final[...] = value
        own[...] = to_own(final)
        start_exchange(own, hood, send, recv)

        def fields_at(sources):
            return [jnp.broadcast_to(near_field[pl.ds(at, 1), :], (8, BLK)) for at in sources]

        for degree, unit_first, units, tile_first in GROUPS:

            def first_body(index, carry, degree=degree, unit_first=unit_first, tile_first=tile_first):
                unit = unit_first + index
                place, half, own_spot, base = unit_at(unit)
                tile = tile_first + index * (3 * degree)
                fields = fields_at(mates(place, half, degree))
                for group in range(16):
                    rows = slice(8 * group, 8 * group + 8)
                    total = tiles[tile, rows, :] * fields[0]
                    for k in range(1, degree):
                        total = total + tiles[tile + k, rows, :] * fields[k]
                    accs[unit, rows, :] = total
                return carry

            lax.fori_loop(0, units, first_body, 0, unroll=2)

        finish_exchange(own, hood, send, recv)

        def field_row(index, carry):
            row = index + SHARE * (index // SHARE)
            near_field[pl.ds(row, 1), :] = hood[pl.ds(field_at[row], 1), :]
            return carry

        lax.fori_loop(0, 2 * SHARE, field_row, 0, unroll=8)

        for degree, unit_first, units, tile_first in GROUPS:

            def unit_body(index, carry, degree=degree, unit_first=unit_first, tile_first=tile_first):
                unit = unit_first + index
                place, half, own_spot, base = unit_at(unit)
                tile = tile_first + index * (3 * degree) + degree
                fields = fields_at(others(place, half, base, degree))
                sums = []
                for group in range(16):
                    rows = slice(8 * group, 8 * group + 8)
                    total = accs[unit, rows, :]
                    for k in range(2 * degree):
                        total = total + tiles[tile + k, rows, :] * fields[k]
                    sums.append(total)
                rowbuf[pl.ds(unit, 1), :] = to_row(jnp.concatenate(sums, axis=0))
                return carry

            lax.fori_loop(0, units, unit_body, 0, unroll=2)

    z = source_at[...] / diag[...]
    product(z, own_z, hood_z, z_send, z_recv)
    y0[...] = settle()
    t = y0[...] / diag[...]
    z = near_field[SHARE : 2 * SHARE, :]
    source = source_at[...]

    def partial(first, second):
        value = jnp.where(mine_here, first * second, 0.0)
        return jnp.sum(jnp.sum(value, axis=0, keepdims=True), axis=1, keepdims=True)

    column_at = lax.broadcasted_iota(jnp.int32, (1, BLK), 1)
    parts_row = jnp.where(column_at == 0, partial(source, z), 0.0)
    parts_row = jnp.where(column_at == 1, partial(z, y0[...]), parts_row)
    parts_row = jnp.where(column_at == 2, partial(y0[...], t), parts_row)
    first_field[...] = z
    product(t, own_t, hood_t, t_send, t_recv)
    y1[...] = settle()
    z = first_field[...]
    t = near_field[SHARE : 2 * SHARE, :]
    moments[0:1, :] = jnp.where(column_at == 3, partial(t, y1[...]), parts_row)

    def share_sums(from_ref, stage, rank, size, member, send, recv):
        copies = []
        for step in range(1, size):
            copy = remote(
                from_ref, stage.at[rank, 0:1, :], send.at[step - 1], recv.at[step - 1], member(lax.rem(rank + step, size))
            )
            copy.start()
            copies.append(copy)
        stage[rank, 0:1, :] = from_ref[...]
        for copy in copies:
            copy.wait()
        total = stage[0, 0:1, :]
        for k in range(1, size):
            total = total + stage[k, 0:1, :]
        return total

    moments[8:9, :] = share_sums(moments.at[0:1, :], stage_a, rank_a, 8, member_a, a_send, a_recv)
    total = share_sums(moments.at[8:9, :], stage_b, chip, 16, member_b, b_send, b_recv)
    e0, e1, e2, e3 = (total[0:1, k : k + 1] for k in range(4))
    f1 = e1 / e0
    f2 = e2 / e0
    f3 = e3 / e0
    lead = 1.0 / (1.0 - f1)
    spread_of = f2 - f1 * f1
    ratio = lead * lead * spread_of
    bent = f3 - 2.0 * f1 * f2 + f1 * f1 * f1
    second = spread_of / (spread_of - bent - lead * spread_of * spread_of)
    mix = ratio - lead * f1
    first_image = y0[...]
    direction = lead * t + mix * z
    source = source_at[...]
    image = (lead - mix) * first_image + mix * source - lead * y1[...]
    final[...] = lead * z + second * direction
    y1[...] = lead * (first_image - f1 * source) - second * image
    x_ref[...] = to_own(final)
    r_ref[...] = to_own(y1)


def body(positions, phase, neighbours, counts, phase_density, right_side):
    pieces = lax.axis_size("piece")
    columns = lax.axis_size("col")
    vmem = pl.BlockSpec(memory_space=pltpu.VMEM)
    smem = pl.BlockSpec(memory_space=pltpu.SMEM)
    f32 = jnp.float32
    dma = pltpu.SemaphoreType.DMA
    shape = jax.ShapeDtypeStruct((SHARE, BLK), f32)
    return pl.pallas_call(
        functools.partial(kernel, pieces, columns),
        out_shape=(shape, shape),
        in_specs=[smem, smem, vmem, vmem, vmem, vmem],
        out_specs=(vmem, vmem),
        scratch_shapes=[
            pltpu.SMEM((LAYER * CELL_STEP,), jnp.int32),
            pltpu.SMEM((LAYER,), jnp.int32),
            pltpu.SMEM((HOOD,), jnp.int32),
            pltpu.SMEM((HOOD,), jnp.int32),
            pltpu.VMEM((4, STATE_NULL + 8, BLK), f32),
            pltpu.VMEM((4, HOOD, BLK), f32),
            pltpu.VMEM((FEATURES * HOOD, BLK), f32),
            pltpu.VMEM((16 * HOOD, BLK), f32),
            pltpu.VMEM((FEATURES * SHARE, BLK), f32),
            pltpu.VMEM((HOOD, FEATURES, 2 * BLK), jnp.bfloat16),
            pltpu.VMEM((SHARE, BLK, FEATURES), jnp.bfloat16),
            pltpu.VMEM((TILES, BLK, BLK), f32),
            pltpu.VMEM((UNITS, BLK, BLK), f32),
            pltpu.VMEM((8, BLK), f32),
            pltpu.VMEM((3, 8, BLK), f32),
            pltpu.VMEM((CAP, BLK), f32),
            pltpu.VMEM((CAP, BLK), f32),
            pltpu.VMEM((4, SHARE, BLK), f32),
            pltpu.VMEM((4, SHARE, BLK), f32),
            pltpu.VMEM((CAP, BLK), f32),
            pltpu.VMEM((SHARE, BLK), f32),
            pltpu.VMEM((SHARE, BLK), f32),
            pltpu.VMEM((FIELD_NULL + 8, BLK), f32),
            pltpu.VMEM((FIELD_NULL + 8, BLK), f32),
            pltpu.VMEM((HOOD, BLK), f32),
            pltpu.VMEM((UNITS, BLK), f32),
            pltpu.VMEM((SHARE, BLK), f32),
            pltpu.VMEM((SHARE, BLK), f32),
            pltpu.VMEM((SHARE, BLK), f32),
            pltpu.VMEM((SHARE, BLK), f32),
            pltpu.VMEM((SHARE, BLK), f32),
            pltpu.VMEM((SHARE, BLK), f32),
            pltpu.VMEM((16, BLK), f32),
            pltpu.VMEM((8, 8, BLK), f32),
            pltpu.VMEM((16, 8, BLK), f32),
            dma((2,)), dma((2,)), dma((3,)), dma((3,)), dma((3,)), dma((3,)),
            dma((6,)), dma((7,)), dma((6,)), dma((7,)),
            dma((7,)), dma((7,)), dma((15,)), dma((15,)),
        ],
        compiler_params=pltpu.CompilerParams(
            collective_id=0, has_side_effects=True, vmem_limit_bytes=60 * 1024 * 1024
        ),
        name="pressure",
    )(counts, phase_density, positions, phase, neighbours.T, right_side)


def solution(mesh):
    placed = (
        P(None, "piece", None),
        P("piece", None),
        P("piece", "col"),
        P(),
        P(),
        P(("piece", "col"), None),
    )
    return jax.shard_map(
        body,
        mesh=mesh,
        in_specs=placed,
        out_specs=(P(("piece", "col"), None), P(("piece", "col"), None)),
        check_vma=False,
    )
```

time: 69 us -> 62.1 us (0.900)
  Pallas kernels: 64.8 us -> 59.2 us
  local copies, waits for them, and re-layouts: 3.34 us -> 1.94 us
    pallas_call x1, Pallas kernels: 64.8 us -> 59.2 us  [body(): pl.pallas_call(functools.partial(kernel, pieces, columns), out_shape=(sha...]
    unnamed x5 -> x4, local copies, waits for them, and re-layouts: 3.34 us -> 1.94 us
where the time goes in v3:
time: 62.1 us; the launch traced here: 61.8 us
  Pallas kernels  59.2 us (95%)
  local copies, waits for them, and re-layouts  1.94 us (3%)
  between operations  0.65 us (1%)
    pallas_call x1, Pallas kernels, body(): pl.pallas_call(functools.partial(kernel, pieces, columns), out_shape=(sha...  59.2 us
    unnamed x4, local copies, waits for them, and re-layouts  1.94 us

profile of v3, /device:TPU:1, one launch (start us, length us, event | category | flops | bytes accessed | tf_op | source)
XLA Modules:
  0.0 61.8 jit_solution(531828140764487277)
XLA Ops:
  0.6 59.2 %pressure.1 = (f32[32,128]{1,0:T(8,128)}, f32[32,128]{1,0:T(8,128)}) custom-call(s32[32]{0:T(128)} %counts.1, f32[3]{0:T(128)} %dens.1, f32[3,128,128]{2,1,0:T(8,128)} %pos_ref.1, s32[128,128]{1,0:T(8,128)} %phase_ref.1, s32[7,128]{1,0:T(8,128)} %bitcast.1, f32[32,128]{1,0:T(8,128)} %rhs_ref.1), custom_call_target="tpu_custom_call" | custom-call | tf_op jit(solution)/shard_map/pressure/pallas_call | solution.py:553
  59.8 0.0 copy-start
  59.8 1.3 %copy.10 = f32[32,128]{1,0:T(8,128)} copy(f32[32,128]{1,0:T(8,128)} %get-tuple-element.4) | data formatting | bytes 32768
  61.1 0.0 copy-done
  61.1 0.6 copy.11
Async XLA Ops:
  59.8 1.3 %copy-start = (f32[32,128]{1,0:T(8,128)S(1)}, f32[32,128]{1,0:T(8,128)}, u32[]{:S(2)}) copy-start(f32[32,128]{1,0:T(8,128)} %get-tuple-element.5) | copy-start | bytes 49156
